TPU v7x, 32 devices: a whole 2x2x4 slice. The times are simulated.
32 devices in a mesh: grp: 2 (over x), probe: 8 (over z, y), beam: 2 (over core).
Axes of the slice: x: 2, y: 2, z: 4, core: 2. Of those that a mesh axis runs over, the one named last changes fastest.
Arguments:
- smatrix: bfloat16 [8192, 8, 512], P(('grp', 'beam'), 'probe'), parts along dimension 0, may hold values from -0.09375 to 0.09375
- aperture: float32 [4096], P('beam'), may hold values from 0.5 to 1.5
- aberration: float32 [4096], P('beam'), may hold values from -3.140625 to 3.140625
- beam_k: int32 [2, 4096], P(None, 'beam'), may hold values from -32 to 31, as said below
- probe_pos: int32 [2, 2048], P(None, 'probe'), may hold values from 0 to 1023
- patches: bfloat16 [128, 512], P(('grp', 'probe')), parts along dimension 0, may hold values from -6 to 6
- patch_col: int32 [128], P('grp'), parts along dimension 0, may hold values from 0 to 7, never falling along the last dimension, each value on 1 to 32 neighbouring positions
Outputs:
- ionization: float32 [16, 2048], P('grp', ('probe', 'beam')), parts along dimension 0
There are 2 independent parts, one for each index of `grp`. A program takes and returns all parts, laid end to end along the dimension named above; an argument that names none is the same for every part. Nothing has to cross between parts.
Inputs may be any that keep to these rules, and one draw needn't show every extreme that they name: `patch_col`: patches are ordered by atom column; each of the 8 columns has 1 to 32 patches, and some column has exactly 32. `beam_k`: no two beams have the same pair of indices.
All inputs are finite; a program needn't handle non-finite values.
Results may differ from a plain program's by a relative error of at most 0.005.
Values may be sent and summed in bfloat16 or wider, within the bound.
A program may use at most 128 MiB of HBM per device.

v0:
```python
import math
import jax
import jax.numpy as jnp
from jax import lax
from jax.sharding import PartitionSpec as P

PSIDE = 16
GRID = 1024


def coefficients(beam_k, aperture, aberration, positions):
    turn_count = jnp.mod(
        positions[0][:, None] * beam_k[0][None, :] + positions[1][:, None] * beam_k[1][None, :],
        GRID,
    )
    phase_angle = aberration[None, :] + 2.0 * math.pi / GRID * turn_count.astype(jnp.float32)
    real_coef = (aperture[None, :] * jnp.cos(phase_angle)).astype(jnp.bfloat16)
    imag_coef = (-(aperture[None, :] * jnp.sin(phase_angle))).astype(jnp.bfloat16)
    return (real_coef, imag_coef)


def detector(edge_count):
    half_side = edge_count // 2
    pixel_index = jnp.arange(edge_count * edge_count, dtype=jnp.int32)
    mode_index = jnp.arange(edge_count * half_side, dtype=jnp.int32)
    row_off = pixel_index // edge_count
    col_off = pixel_index % edge_count
    freq_first = mode_index // half_side - half_side
    freq_second = mode_index % half_side - edge_count // 4
    turn_count = jnp.mod(
        row_off[:, None] * freq_first[None, :] + col_off[:, None] * freq_second[None, :], edge_count
    )
    angle_value = 2.0 * math.pi / edge_count * turn_count.astype(jnp.float32)
    real_part = jnp.cos(angle_value)
    imag_part = -jnp.sin(angle_value)
    upper_rows = jnp.concatenate([real_part, imag_part], axis=1)
    lower_rows = jnp.concatenate([-imag_part, real_part], axis=1)
    return jnp.concatenate([upper_rows, lower_rows], axis=0).astype(jnp.bfloat16)


def patch_energy(picked, pot_rows, det_table):
    half_width = pot_rows.shape[-1] // 2
    psi_re = picked[..., :half_width].astype(jnp.float32)
    psi_im = picked[..., half_width:].astype(jnp.float32)
    pot_re = pot_rows[:, :half_width].astype(jnp.float32)
    pot_im = pot_rows[:, half_width:].astype(jnp.float32)
    wave_out = jnp.concatenate(
        [psi_re * pot_re - psi_im * pot_im, psi_re * pot_im + psi_im * pot_re], axis=-1
    ).astype(jnp.bfloat16)
    projected = jnp.einsum("rjx,xq->rjq", wave_out, det_table, preferred_element_type=jnp.float32)
    return jnp.sum(projected * projected, axis=-1) / float(half_width * (det_table.shape[1] // 2))


def combine(beam_terms):
    half_width = beam_terms.shape[-1] // 2
    return jnp.concatenate(
        [
            beam_terms[0, ..., :half_width] - beam_terms[1, ..., half_width:],
            beam_terms[0, ..., half_width:] + beam_terms[1, ..., :half_width],
        ],
        axis=-1,
    )


def spread_patches(psi, all_patches, patch_col, det_table):
    patch_total = all_patches.shape[0]
    group_size = math.gcd(patch_total, 16)
    column_count = psi.shape[1]
    col_groups = patch_col.reshape(patch_total // group_size, group_size)
    pot_groups = all_patches.reshape(patch_total // group_size, group_size, all_patches.shape[1])
    col_range = jnp.arange(column_count, dtype=jnp.int32)

    def add_block(running, blk_pair):
        col_ids, pot_rows = blk_pair
        picked = jnp.take(psi, col_ids, axis=1)
        energy = patch_energy(picked, pot_rows, det_table)
        onehot = (col_ids[:, None] == col_range[None, :]).astype(jnp.float32)
        return (
            running + jnp.einsum("rj,jc->cr", energy, onehot, precision=lax.Precision.HIGHEST),
            None,
        )

    running, _ = lax.scan(
        add_block, jnp.zeros((column_count, psi.shape[0]), jnp.float32), (col_groups, pot_groups)
    )
    return running


def apply_patches(psi_own, all_patches, patch_col, det_table):
    traded = lax.all_to_all(psi_own, "probe", split_axis=0, concat_axis=2, tiled=True)
    return spread_patches(traded[0], all_patches, patch_col, det_table)


def shards(smatrix, aperture, aberration, beam_k, probe_pos, patches, patch_col):
    probe_count = lax.axis_size("probe")
    beam_count = lax.axis_size("beam")
    all_patches = lax.all_gather(patches, "probe", axis=0, tiled=True)
    det_table = detector(PSIDE)
    col_dev = smatrix.shape[1]
    width_two = smatrix.shape[2]
    full_matrix, full_aperture, full_aberration, full_k = (
        lax.all_gather(smatrix, "beam", axis=0, tiled=True),
        lax.all_gather(aperture.astype(jnp.bfloat16), "beam", axis=0, tiled=True).astype(
            aperture.dtype
        ),
        lax.all_gather(aberration.astype(jnp.bfloat16), "beam", axis=0, tiled=True).astype(
            aberration.dtype
        ),
        lax.all_gather(beam_k, "beam", axis=1, tiled=True),
    )
    all_pos = lax.all_gather(probe_pos, "probe", axis=1, tiled=True)
    probe_total = all_pos.shape[1]
    half_probes = probe_total // (beam_count * probe_count)
    split_pos = all_pos.reshape(2, probe_count, beam_count, half_probes)
    mine = lax.dynamic_slice_in_dim(split_pos, lax.axis_index("beam"), 1, 2).reshape(
        2, probe_count * half_probes
    )
    row_total = probe_count * half_probes
    block_rows = math.gcd(row_total, 512)
    pos_blocks = mine.reshape(2, row_total // block_rows, block_rows).transpose(1, 0, 2)

    def whole_block(positions):
        real_coef, imag_coef = coefficients(full_k, full_aperture, full_aberration, positions)
        beam_terms = jnp.einsum(
            "kpb,bcx->kpcx",
            jnp.stack([real_coef, imag_coef]),
            full_matrix,
            preferred_element_type=jnp.float32,
        )
        return combine(beam_terms).astype(jnp.bfloat16)

    psi_own = lax.map(whole_block, pos_blocks).reshape(probe_count, half_probes, col_dev, width_two)
    return apply_patches(psi_own, all_patches, patch_col, det_table)


def solution(mesh):
    placed = (
        P(("grp", "beam"), "probe", None),
        P("beam"),
        P("beam"),
        P(None, "beam"),
        P(None, "probe"),
        P(("grp", "probe"), None),
        P("grp"),
    )
    return jax.shard_map(
        shards, mesh=mesh, in_specs=placed, out_specs=P("grp", ("probe", "beam")), check_vma=False
    )
```

profile of v0, /device:TPU:0, one launch (start us, length us, event | category | flops | bytes accessed | tf_op | source)
XLA Modules:
  0.0 199.8 jit_solution(7711247507291517825)
XLA Ops:
  6.6 4.0 %copy.15 = bf16[2048,1,512]{0,2,1:T(8,128)(2,1)} copy(bf16[2048,1,512]{2,0,1:T(8,128)(2,1)} %param.11) | data formatting | bytes 4194304 | tf_op args[0]
  10.6 2.0 all_gather.18
  12.6 1.8 all_gather.19
  14.4 27.8 %all_gather.20 = s32[2,2048]{1,0:T(2,128)S(1)} all-gather(s32[2,256]{1,0:T(2,128)S(1)} %copy-done.5), channel_id=1, replica_groups=mesh['grp'=2,'probe'=8,'beam'=2] {'probe'}, dimensions={1}, use_global_device_ids=true | all-gather | bytes 18432 | tf_op jit(solution)/shard_map/all_gather | solution.py:111
  42.3 1.8 all_gather.21
  44.2 82.0 %while.23 = (s32[]{:T(128)}, bf16[2,512,1,512]{3,1,0,2:T(8,128)(2,1)}, f32[4096]{0:T(1024)S(1)}, f32[4096]{0:T(1024)S(1)}, s32[2,2,512]{2,0,1:T(2,128)S(1)}, /*i...) while((s32[]{:T(128)}, bf16[2,512,1,512]{3,1,0,2:T(8,128)(2,1)}, ...), condition=%wide.region_1.2_spmd, body=%wide.region_0.1_spmd.sunk | while | flops 4346871808 | bytes 45756576 | solution.py:132
  44.3 35.1 %multiply_convert_fusion.2 = (bf16[1,512,4096]{2,1,0:T(8,128)(2,1)S(1)}, bf16[1,512,4096]{2,1,0:T(8,128)(2,1)S(1)}) fusion(s32[4096]{0:T(1024)S(1)} %bitcast.69, s32[512]{0:T(512)S(1)} %bitcast.72, s32[4096]{0:T(1024)S(1)} %bitcast.68, s32[512]{0:T(512)S(1)} %bitcast.71, f32[4096]{0:T(1024)S(1)} %get-tuple-element.349, f32[4096]{0:T(1024)S(1)} %get-tuple-element.348), kind=kLoop, calls=%fused_computation.14.clone.1 | loop fusion | flops 46137344 | bytes 8458240 | tf_op jit(solution)/shard_map/while/body/eval_jaxpr/convert_element_type | solution.py:17
  79.4 4.5 %fusion.66 = f32[2,512,1,512]{1,3,0,2:T(8,128)S(1)} fusion(bf16[4096,1,512]{0,2,1:T(8,128)(2,1)S(1)} %copy-done.7, bf16[1,512,4096]{2,1,0:T(8,128)(2,1)S(1)} %get-tuple-element.310, bf16[1,512,4096]{2,1,0:T(8,128)(2,1)S(1)} %get-tuple-element.311), kind=kOutput, calls=%fused_computation.16.clone.1 | convolution fusion | flops 4299161600 | bytes 14680064 | tf_op jit(solution)/shard_map/while/body/eval_jaxpr/kpb,bcx->kpcx/dot_general | solution.py:124
  84.4 0.8 constant_dynamic-update-slice_fusion.2
  85.3 35.1 %multiply_convert_fusion.2 = (bf16[1,512,4096]{2,1,0:T(8,128)(2,1)S(1)}, bf16[1,512,4096]{2,1,0:T(8,128)(2,1)S(1)}) fusion(s32[4096]{0:T(1024)S(1)} %bitcast.69, s32[512]{0:T(512)S(1)} %bitcast.72, s32[4096]{0:T(1024)S(1)} %bitcast.68, s32[512]{0:T(512)S(1)} %bitcast.71, f32[4096]{0:T(1024)S(1)} %get-tuple-element.349, f32[4096]{0:T(1024)S(1)} %get-tuple-element.348), kind=kLoop, calls=%fused_computation.14.clone.1 | loop fusion | flops 46137344 | bytes 8458240 | tf_op jit(solution)/shard_map/while/body/eval_jaxpr/convert_element_type | solution.py:17
  120.4 4.5 %fusion.66 = f32[2,512,1,512]{1,3,0,2:T(8,128)S(1)} fusion(bf16[4096,1,512]{0,2,1:T(8,128)(2,1)S(1)} %copy-done.7, bf16[1,512,4096]{2,1,0:T(8,128)(2,1)S(1)} %get-tuple-element.310, bf16[1,512,4096]{2,1,0:T(8,128)(2,1)S(1)} %get-tuple-element.311), kind=kOutput, calls=%fused_computation.16.clone.1 | convolution fusion | flops 4299161600 | bytes 14680064 | tf_op jit(solution)/shard_map/while/body/eval_jaxpr/kpb,bcx->kpcx/dot_general | solution.py:124
  125.4 0.8 constant_dynamic-update-slice_fusion.2
  126.2 4.0 %all-to-all-start = ((bf16[8,128,1,512]{3,1,2,0:T(8,128)(2,1)}), bf16[8,128,1,512]{3,1,2,0:T(8,128)(2,1)S(1)}, u32[]{:S(2)}, u32[]{:S(2)}) async-start(bf16[8,128,1,512]{3,1,2,0:T(8,128)(2,1)} %bitcast.9), calls=%async_computation | async-start | bytes 2097152 | tf_op jit(solution)/shard_map/all_to_all | solution.py:90
  130.3 46.0 %all_gather.23 = bf16[64,512]{1,0:T(8,128)(2,1)S(1)} all-gather(bf16[8,512]{1,0:T(8,128)(2,1)S(1)} %copy-done.2), channel_id=1, replica_groups=mesh['grp'=2,'probe'=8,'beam'=2] {'probe'}, dimensions={0}, use_global_device_ids=true | all-gather | bytes 73728 | tf_op jit(solution)/shard_map/all_gather | solution.py:97
  177.0 15.3 %while.24 = (s32[]{:T(128)}, f32[8,128]{1,0:T(8,128)S(1)}, s32[4,16]{1,0:T(4,128)S(1)}, bf16[128,8,512]{2,0,1:T(8,128)(2,1)S(1)}, bf16[4,16,512]{2,1,0:T(8,128)(...) while((s32[]{:T(128)}, f32[8,128]{1,0:T(8,128)S(1)}, s32[4,16]{1,0:T(4,128)S(1)}, ...), condition=%wide.region_4.5_spmd.clone, body=%wide.region_2.4_spmd.clone.sunk | while | flops 548613504 | bytes 15086163 | solution.py:83
  177.1 0.7 gather_fusion
  177.8 1.3 fusion.73
  179.1 0.7 fusion.74
  179.8 0.8 multiply_reduce_fusion.2
  180.9 0.7 gather_fusion
  181.7 1.3 fusion.73
  182.9 0.7 fusion.74
  183.6 0.8 multiply_reduce_fusion.2
  184.8 0.7 gather_fusion
  185.5 1.3 fusion.73
  186.8 0.7 fusion.74
  187.5 0.8 multiply_reduce_fusion.2
  188.6 0.7 gather_fusion
  189.3 1.3 fusion.73
  190.6 0.7 fusion.74
  191.3 0.8 multiply_reduce_fusion.2
  192.3 0.7 copy-done
  (69 shorter events, 3.1 us)
Async XLA Ops:
  6.5 4.1 %copy-start.3 = (f32[2048]{0:T(1024)S(1)}, f32[2048]{0:T(1024)}, u32[]{:S(2)}) copy-start(f32[2048]{0:T(1024)} %param.12) | copy-start | bytes 24580
  6.5 6.1 %copy-start.4 = (f32[2048]{0:T(1024)S(1)}, f32[2048]{0:T(1024)}, u32[]{:S(2)}) copy-start(f32[2048]{0:T(1024)} %param.13) | copy-start | bytes 24580
  6.5 7.9 %copy-start.5 = (s32[2,256]{1,0:T(2,128)S(1)}, s32[2,256]{1,0:T(2,128)}, u32[]{:S(2)}) copy-start(s32[2,256]{1,0:T(2,128)} %param.15) | copy-start | bytes 6148
  6.5 35.8 %copy-start.1 = (s32[2,2048]{1,0:T(2,128)S(1)}, s32[2,2048]{1,0:T(2,128)}, u32[]{:S(2)}) copy-start(s32[2,2048]{1,0:T(2,128)} %param.14) | copy-start | bytes 49156
  6.5 37.6 %all-gather.2.cloned.1.call-start = ((), (), s32[]{:S(2)}) async-start(), calls=%async_computation.1 | async-start | bytes 6291456 | tf_op jit(solution)/shard_map/all_gather | solution.py:102
  44.2 86.0 %copy-start.6 = (s32[64]{0:T(128)S(1)}, s32[64]{0:T(128)}, u32[]{:S(2)}) copy-start(s32[64]{0:T(128)} %param.17) | copy-start | bytes 772
  44.2 86.1 %copy-start.2 = (bf16[8,512]{1,0:T(8,128)(2,1)S(1)}, bf16[8,512]{1,0:T(8,128)(2,1)}, u32[]{:S(2)}) copy-start(bf16[8,512]{1,0:T(8,128)(2,1)} %param.16) | copy-start | bytes 24580
  44.3 35.1 %copy-start.7 = (bf16[4096,1,512]{0,2,1:T(8,128)(2,1)S(1)}, bf16[4096,1,512]{0,2,1:T(8,128)(2,1)}, u32[]{:S(2)}) copy-start(bf16[4096,1,512]{0,2,1:T(8,128)(2,1)} %get-tuple-element.352) | copy-start | bytes 12582916 | tf_op jit(solution)/shard_map/while
  85.3 35.1 %copy-start.7 = (bf16[4096,1,512]{0,2,1:T(8,128)(2,1)S(1)}, bf16[4096,1,512]{0,2,1:T(8,128)(2,1)}, u32[]{:S(2)}) copy-start(bf16[4096,1,512]{0,2,1:T(8,128)(2,1)} %get-tuple-element.352) | copy-start | bytes 12582916 | tf_op jit(solution)/shard_map/while
  126.2 50.8 %all-to-all-start = ((bf16[8,128,1,512]{3,1,2,0:T(8,128)(2,1)}), bf16[8,128,1,512]{3,1,2,0:T(8,128)(2,1)S(1)}, u32[]{:S(2)}, u32[]{:S(2)}) async-start(bf16[8,128,1,512]{3,1,2,0:T(8,128)(2,1)} %bitcast.9), calls=%async_computation | async-start | bytes 2097152 | tf_op jit(solution)/shard_map/all_to_all | solution.py:90
  192.3 0.7 copy-start
Sparse Core Ops, SparseCore 0:
  10.7 16.3 all-gather.1
where the time goes:
time: 200 us
  other arithmetic  79.6 us (40%)
  blocking collectives  79.5 us (40%)
  between operations  13.5 us (7%)
  matrix products  13.1 us (7%)
  local copies, waits for them, and re-layouts  9.73 us (5%)
  starting transfers between devices  4.03 us (2%)
    convert_element_type x2, other arithmetic, coefficients(): real_coef = (aperture[None, :] * jnp.cos(phase_angle)).astype(jnp.bfloat16)  70.2 us
    all_gather x1, blocking collectives, shards(): all_patches = lax.all_gather(patches, 'probe', axis=0, tiled=True)  46 us
    all_gather x1, blocking collectives, shards(): all_pos = lax.all_gather(probe_pos, 'probe', axis=1, tiled=True)  27.8 us
    dot_general x2, matrix products, whole_block(): jnp.einsum('kpb,bcx->kpcx', jnp.stack([real_coef, imag_coef]), full_matri...  9.05 us
    select_n x8, other arithmetic, add_block(): picked = jnp.take(psi, col_ids, axis=1)  5.19 us
    unnamed x15, local copies, waits for them, and re-layouts  4.67 us
  transfers between devices with their start and end apart: 2, of which 0 were waited for; matrix products, arithmetic and copies ran while one was open for 0% of the time, Pallas kernels for 0%

commit v1 on v0

--- a/solution.py
+++ b/solution.py
@@ -87,7 +87,12 @@
 
 
 def apply_patches(psi_own, all_patches, patch_col, det_table):
-    traded = lax.all_to_all(psi_own, "probe", split_axis=0, concat_axis=2, tiled=True)
+    traded = jnp.concatenate(
+        lax.all_to_all(
+            jnp.stack(jnp.split(psi_own, lax.axis_size("probe"), axis=0)), "probe", 0, 0
+        ),
+        axis=2,
+    )
     return spread_patches(traded[0], all_patches, patch_col, det_table)
 
 

time: 200 us -> 204 us (1.020)
  local copies, waits for them, and re-layouts: 9.73 us -> 13.4 us
    unnamed x15 -> x22, local copies, waits for them, and re-layouts: 4.67 us -> 9.28 us
where the time goes in v1:
time: 204 us
  other arithmetic  79.5 us (39%)
  blocking collectives  79.5 us (39%)
  between operations  13.5 us (7%)
  local copies, waits for them, and re-layouts  13.4 us (7%)
  matrix products  13.1 us (6%)
  starting transfers between devices  4.03 us (2%)
    convert_element_type x2, other arithmetic, coefficients(): real_coef = (aperture[None, :] * jnp.cos(phase_angle)).astype(jnp.bfloat16)  70.3 us
    all_gather x1, blocking collectives, shards(): all_patches = lax.all_gather(patches, 'probe', axis=0, tiled=True)  46.1 us
    all_gather x1, blocking collectives, shards(): all_pos = lax.all_gather(probe_pos, 'probe', axis=1, tiled=True)  27.9 us
    unnamed x22, local copies, waits for them, and re-layouts  9.28 us
    dot_general x2, matrix products, whole_block(): jnp.einsum('kpb,bcx->kpcx', jnp.stack([real_coef, imag_coef]), full_matri...  9.05 us
    select_n x8, other arithmetic, add_block(): picked = jnp.take(psi, col_ids, axis=1)  5.24 us
  transfers between devices with their start and end apart: 2, of which 0 were waited for; matrix products, arithmetic and copies ran while one was open for 0% of the time, Pallas kernels for 0%

profile of v1, /device:TPU:0, one launch (start us, length us, event | category | flops | bytes accessed | tf_op | source)
XLA Modules:
  0.0 203.8 jit_solution(8432644469660937466)
XLA Ops:
  6.6 4.0 %copy.23 = bf16[2048,1,512]{0,2,1:T(8,128)(2,1)} copy(bf16[2048,1,512]{2,0,1:T(8,128)(2,1)} %param.11) | data formatting | bytes 4194304 | tf_op args[0]
  10.6 27.9 %all_gather.20 = s32[2,2048]{1,0:T(2,128)S(1)} all-gather(s32[2,256]{1,0:T(2,128)S(1)} %copy-done.5), channel_id=1, replica_groups=mesh['grp'=2,'probe'=8,'beam'=2] {'probe'}, dimensions={1}, use_global_device_ids=true | all-gather | bytes 18432 | tf_op jit(solution)/shard_map/all_gather | solution.py:116
  38.6 1.8 all_gather.18
  40.5 1.8 all_gather.19
  42.3 1.8 all_gather.21
  44.2 80.7 %while.23 = (s32[]{:T(128)}, bf16[2,512,1,512]{3,1,0,2:T(8,128)(2,1)S(1)}, f32[4096]{0:T(1024)S(1)}, f32[4096]{0:T(1024)S(1)}, s32[2,2,512]{2,0,1:T(2,128)S(1)},...) while((s32[]{:T(128)}, ...), condition=%wide.region_1.2_spmd, body=%wide.region_0.1_spmd.sunk | while | flops 4346871808 | bytes 45756568 | solution.py:137
  44.2 35.1 %multiply_convert_fusion.2 = (bf16[1,512,4096]{2,1,0:T(8,128)(2,1)S(1)}, bf16[1,512,4096]{2,1,0:T(8,128)(2,1)S(1)}) fusion(s32[4096]{0:T(1024)S(1)} %bitcast.97, s32[512]{0:T(512)S(1)} %bitcast.108, s32[4096]{0:T(1024)S(1)} %bitcast.96, s32[512]{0:T(512)S(1)} %bitcast.107, f32[4096]{0:T(1024)S(1)} %get-tuple-element.349, f32[4096]{0:T(1024)S(1)} %get-tuple-element.348), kind=kLoop, calls=%fused_computation.14.clone.1 | loop fusion | flops 46137344 | bytes 8458240 | tf_op jit(solution)/shard_map/while/body/eval_jaxpr/convert_element_type | solution.py:17
  79.4 4.5 %fusion.74 = f32[2,512,1,512]{1,3,0,2:T(8,128)S(1)} fusion(bf16[4096,1,512]{0,2,1:T(8,128)(2,1)S(1)} %copy-done.7, bf16[1,512,4096]{2,1,0:T(8,128)(2,1)S(1)} %get-tuple-element.310, bf16[1,512,4096]{2,1,0:T(8,128)(2,1)S(1)} %get-tuple-element.311), kind=kOutput, calls=%fused_computation.16.clone.1 | convolution fusion | flops 4299161600 | bytes 14680064 | tf_op jit(solution)/shard_map/while/body/eval_jaxpr/kpb,bcx->kpcx/dot_general | solution.py:129
  84.5 35.1 %multiply_convert_fusion.2 = (bf16[1,512,4096]{2,1,0:T(8,128)(2,1)S(1)}, bf16[1,512,4096]{2,1,0:T(8,128)(2,1)S(1)}) fusion(s32[4096]{0:T(1024)S(1)} %bitcast.97, s32[512]{0:T(512)S(1)} %bitcast.108, s32[4096]{0:T(1024)S(1)} %bitcast.96, s32[512]{0:T(512)S(1)} %bitcast.107, f32[4096]{0:T(1024)S(1)} %get-tuple-element.349, f32[4096]{0:T(1024)S(1)} %get-tuple-element.348), kind=kLoop, calls=%fused_computation.14.clone.1 | loop fusion | flops 46137344 | bytes 8458240 | tf_op jit(solution)/shard_map/while/body/eval_jaxpr/convert_element_type | solution.py:17
  119.6 4.5 %fusion.74 = f32[2,512,1,512]{1,3,0,2:T(8,128)S(1)} fusion(bf16[4096,1,512]{0,2,1:T(8,128)(2,1)S(1)} %copy-done.7, bf16[1,512,4096]{2,1,0:T(8,128)(2,1)S(1)} %get-tuple-element.310, bf16[1,512,4096]{2,1,0:T(8,128)(2,1)S(1)} %get-tuple-element.311), kind=kOutput, calls=%fused_computation.16.clone.1 | convolution fusion | flops 4299161600 | bytes 14680064 | tf_op jit(solution)/shard_map/while/body/eval_jaxpr/kpb,bcx->kpcx/dot_general | solution.py:129
  127.5 0.7 fusion.46
  128.8 0.7 fusion.44
  129.5 0.7 fusion.43
  130.1 4.0 %all-to-all-start = ((bf16[8,1,128,1,512]{4,2,3,1,0:T(8,128)(2,1)}), bf16[8,1,128,1,512]{4,2,3,1,0:T(8,128)(2,1)S(1)}, u32[]{:S(2)}, u32[]{:S(2)}) async-start(bf16[8,1,128,1,512]{4,2,3,1,0:T(8,128)(2,1)} %fusion.43), calls=%async_computation | async-start | bytes 2097152 | tf_op jit(solution)/shard_map/all_to_all | solution.py:91
  134.2 46.1 %all_gather.23 = bf16[64,512]{1,0:T(8,128)(2,1)S(1)} all-gather(bf16[8,512]{1,0:T(8,128)(2,1)S(1)} %copy-done.2), channel_id=1, replica_groups=mesh['grp'=2,'probe'=8,'beam'=2] {'probe'}, dimensions={0}, use_global_device_ids=true | all-gather | bytes 73728 | tf_op jit(solution)/shard_map/all_gather | solution.py:102
  181.0 15.3 %while.24 = (s32[]{:T(128)}, f32[8,128]{1,0:T(8,128)S(1)}, s32[4,16]{1,0:T(4,128)S(1)}, bf16[128,8,512]{2,0,1:T(8,128)(2,1)S(1)}, bf16[4,16,512]{2,1,0:T(8,128)(...) while((s32[]{:T(128)}, f32[8,128]{1,0:T(8,128)S(1)}, s32[4,16]{1,0:T(4,128)S(1)}, ...), condition=%wide.region_4.5_spmd.clone, body=%wide.region_2.4_spmd.clone.sunk | while | flops 548613504 | bytes 15086155 | solution.py:83
  181.0 0.7 gather_fusion
  181.7 1.3 fusion.81
  183.1 0.7 fusion.82
  183.8 0.8 multiply_reduce_fusion.2
  184.9 0.7 gather_fusion
  185.6 1.3 fusion.81
  186.9 0.7 fusion.82
  187.6 0.8 multiply_reduce_fusion.2
  188.7 0.7 gather_fusion
  189.4 1.3 fusion.81
  190.7 0.7 fusion.82
  191.4 0.8 multiply_reduce_fusion.2
  192.5 0.7 gather_fusion
  193.2 1.3 fusion.81
  194.6 0.7 fusion.82
  195.3 0.8 multiply_reduce_fusion.2
  (77 shorter events, 7.0 us)
Async XLA Ops:
  6.5 4.1 %copy-start.5 = (s32[2,256]{1,0:T(2,128)S(1)}, s32[2,256]{1,0:T(2,128)}, u32[]{:S(2)}) copy-start(s32[2,256]{1,0:T(2,128)} %param.15) | copy-start | bytes 6148
  6.5 32.1 %copy-start.3 = (f32[2048]{0:T(1024)S(1)}, f32[2048]{0:T(1024)}, u32[]{:S(2)}) copy-start(f32[2048]{0:T(1024)} %param.12) | copy-start | bytes 24580
  6.5 33.9 %copy-start.4 = (f32[2048]{0:T(1024)S(1)}, f32[2048]{0:T(1024)}, u32[]{:S(2)}) copy-start(f32[2048]{0:T(1024)} %param.13) | copy-start | bytes 24580
  6.5 35.8 %copy-start.1 = (s32[2,2048]{1,0:T(2,128)S(1)}, s32[2,2048]{1,0:T(2,128)}, u32[]{:S(2)}) copy-start(s32[2,2048]{1,0:T(2,128)} %param.14) | copy-start | bytes 49156
  6.5 37.6 %all-gather.2.cloned.1.call-start = ((), (), s32[]{:S(2)}) async-start(), calls=%async_computation.1 | async-start | bytes 6291456 | tf_op jit(solution)/shard_map/all_gather | solution.py:107
  44.2 35.2 %copy-start.7 = (bf16[4096,1,512]{0,2,1:T(8,128)(2,1)S(1)}, bf16[4096,1,512]{0,2,1:T(8,128)(2,1)}, u32[]{:S(2)}) copy-start(bf16[4096,1,512]{0,2,1:T(8,128)(2,1)} %get-tuple-element.352) | copy-start | bytes 12582916 | tf_op jit(solution)/shard_map/while
  84.5 35.2 %copy-start.7 = (bf16[4096,1,512]{0,2,1:T(8,128)(2,1)S(1)}, bf16[4096,1,512]{0,2,1:T(8,128)(2,1)}, u32[]{:S(2)}) copy-start(bf16[4096,1,512]{0,2,1:T(8,128)(2,1)} %get-tuple-element.352) | copy-start | bytes 12582916 | tf_op jit(solution)/shard_map/while
  124.8 9.3 %copy-start.6 = (s32[64]{0:T(128)S(1)}, s32[64]{0:T(128)}, u32[]{:S(2)}) copy-start(s32[64]{0:T(128)} %param.17) | copy-start | bytes 772
  124.8 9.4 %copy-start.2 = (bf16[8,512]{1,0:T(8,128)(2,1)S(1)}, bf16[8,512]{1,0:T(8,128)(2,1)}, u32[]{:S(2)}) copy-start(bf16[8,512]{1,0:T(8,128)(2,1)} %param.16) | copy-start | bytes 24580
  130.1 50.9 %all-to-all-start = ((bf16[8,1,128,1,512]{4,2,3,1,0:T(8,128)(2,1)}), bf16[8,1,128,1,512]{4,2,3,1,0:T(8,128)(2,1)S(1)}, u32[]{:S(2)}, u32[]{:S(2)}) async-start(bf16[8,1,128,1,512]{4,2,3,1,0:T(8,128)(2,1)} %fusion.43), calls=%async_computation | async-start | bytes 2097152 | tf_op jit(solution)/shard_map/all_to_all | solution.py:91
  196.3 0.7 copy-start
Sparse Core Ops, SparseCore 0:
  10.7 16.3 all-gather.1
